TPU v7x, 32 devices: a whole 2x2x4 slice. The times are simulated.
32 devices in a mesh: dp: 16 (over z, x, core), vol: 2 (over y).
Axes of the slice: x: 2, y: 2, z: 4, core: 2. Of those that a mesh axis runs over, the one named last changes fastest.
Arguments:
- images: float32 [32, 128, 128], P(('dp', 'vol')), may hold values from -6 to 6
- contrast: bfloat16 [32, 128, 128], P(('dp', 'vol')), may hold values from -1 to 1
- volume: bfloat16 [256, 256, 256], P('vol'), may hold values from -6 to 6
- line_index: int32 [32, 4, 128], P('dp'), may hold values from 0 to 65278, as said below
- patch_weight: bfloat16 [64, 1024], replicated, may hold values from -0.75 to 0.75
- position: bfloat16 [256, 1024], replicated, may hold values from -3 to 3
- norm_gain: float32 [1024], replicated, may hold values from 0.1 to 1.9
- project_in: bfloat16 [1024, 1536], P('dp'), may hold values from -0.1875 to 0.1875
- project_out: bfloat16 [1024, 512], P('dp'), may hold values from -0.25 to 0.25
- head_weight: float32 [1024, 4], replicated, may hold values from -1.8 to 1.8
Outputs:
- errors: float32 [32, 4], P(('dp', 'vol'))
- in_gradient: float32 [1024, 1536], P('dp')
- out_gradient: float32 [1024, 512], P('dp')
- head_gradient: float32 [1024, 4], replicated
Inputs may be any that keep to these rules, and one draw needn't show every extreme that they name: line_index[i, k, r] = z * 256 + y names the plane z and row y of the volume that row r of hypothesis k of image i samples; z and y lie within 0 and 254.
All inputs are finite; a program needn't handle non-finite values.
Results may differ from a plain program's by a relative error of at most 0.038.
Values may be sent and summed in bfloat16 or wider, within the bound.
A program may use at most 64 MiB of HBM per device.

v0:
```python
import math
import jax
import jax.numpy as jnp
from jax import lax
from jax.sharding import PartitionSpec as P

HEADS = 8
HEAD_DIM = 64
PIX = 128
PATCH = 8
PATCHES = 256
K = 4
EPSILON = 1e-05


def embed_images(images, patch_weight, position):
    count = images.shape[0]
    grid = PIX // PATCH
    pieces = images.reshape(count, grid, PATCH, grid, PATCH).transpose(0, 1, 3, 2, 4)
    pieces = pieces.reshape(count * grid * grid, PATCH * PATCH).astype(jnp.bfloat16)
    mixed = jnp.dot(pieces, patch_weight, preferred_element_type=jnp.float32)
    mixed = mixed.reshape(count, grid * grid, -1) + position.astype(jnp.float32)[None]
    return mixed.reshape(count * grid * grid, -1).astype(jnp.bfloat16)


def normalize(embedded, norm_gain):
    values = embedded.astype(jnp.float32)
    center = values - jnp.mean(values, axis=1, keepdims=True)
    scale = lax.rsqrt(jnp.mean(center * center, axis=1, keepdims=True) + EPSILON)
    return (center * scale * norm_gain[None, :]).astype(jnp.bfloat16)


def attend(triple):
    count = triple.shape[0] // PATCHES
    parts = triple.reshape(count, PATCHES, 3, HEADS, HEAD_DIM).astype(jnp.float32)
    query = parts[:, :, 0]
    keys = parts[:, :, 1]
    values = parts[:, :, 2]
    scores = jnp.einsum("bqhd,bkhd->bhqk", query, keys) * HEAD_DIM ** (-0.5)
    raised = jnp.exp(scores)
    weights = (raised / jnp.sum(raised, axis=-1, keepdims=True)).astype(jnp.bfloat16)
    mixed = jnp.einsum("bhqk,bkhd->bqhd", weights.astype(jnp.float32), values)
    return mixed.reshape(count * PATCHES, HEADS * HEAD_DIM).astype(jnp.bfloat16)


def hartley(images):
    side = images.shape[1]
    freq = jnp.arange(side, dtype=jnp.int32) - side // 2
    place = jnp.arange(side, dtype=jnp.int32)
    phase = (freq[:, None] * place[None, :] % side).astype(jnp.float32) * (2.0 * math.pi / side)
    cosine = jnp.cos(phase)
    sine = jnp.sin(phase)
    highest = lax.Precision.HIGHEST
    first_cos = jnp.einsum("rn,bnm->brm", cosine, images, precision=highest)
    first_sin = jnp.einsum("rn,bnm->brm", sine, images, precision=highest)
    result = jnp.einsum("brm,cm->brc", first_cos, cosine + sine, precision=highest)
    result = result + jnp.einsum("brm,cm->brc", first_sin, cosine - sine, precision=highest)
    return result / side


def render(volume, line_index, slab_index):
    slab, side, _ = volume.shape
    table = volume.reshape(slab * side, side)
    plane = line_index // side - slab_index * slab
    inside = (plane >= 0) & (plane < slab)
    rows = jnp.clip(plane, 0, slab - 1) * side + line_index % side
    picked = jnp.take(table, rows.reshape(-1), axis=0)[:, ::2]
    picked = jnp.where(inside.reshape(-1, 1), picked.astype(jnp.float32), 0.0)
    return (picked.reshape(line_index.shape[0], -1), inside)


def local(
    images,
    contrast,
    volume,
    line_index,
    patch_weight,
    position,
    norm_gain,
    project_in,
    project_out,
    head_weight,
):
    count = images.shape[0]
    width = norm_gain.shape[0]
    highest = lax.Precision.HIGHEST
    rendered, inside = render(volume, line_index, lax.axis_index("vol"))
    spectrum = hartley(images)
    slices = lax.psum_scatter(
        rendered.astype(jnp.bfloat16), "vol", scatter_dimension=0, tiled=True
    ).astype(jnp.float32)
    slices = slices.reshape(count, K, PIX, PIX)
    misfit = contrast.astype(jnp.float32)[:, None] * slices - spectrum[:, None]
    errors = jnp.mean(misfit * misfit, axis=(2, 3))
    embedded = embed_images(images, patch_weight, position)
    normed = normalize(embedded, norm_gain)
    triple = jnp.dot(
        normed,
        lax.all_gather(project_in, "dp", axis=0, tiled=True),
        preferred_element_type=jnp.float32,
    ).astype(jnp.bfloat16)
    attended = attend(triple)
    contract_last = (((1,), (1,)), ((), ()))
    out_whole = lax.all_gather(project_out, "dp", axis=0, tiled=True)
    branch = lax.dot_general(attended, out_whole, contract_last, preferred_element_type=jnp.float32)
    layer_out = embedded.astype(jnp.float32) + branch
    pooled = jnp.mean(layer_out.reshape(count, PATCHES, width), axis=1)
    logits = jnp.dot(pooled, head_weight, precision=highest)
    raised = jnp.exp(logits)
    chances = raised / jnp.sum(raised, axis=1, keepdims=True)
    expected = jnp.sum(chances * errors, axis=1, keepdims=True)
    logit_slope = chances * (errors - expected)
    head_gradient = lax.psum(jnp.dot(pooled.T, logit_slope, precision=highest), ("dp", "vol"))
    pooled_slope = jnp.dot(logit_slope, head_weight.T, precision=highest) / PATCHES
    layer_slope = jnp.broadcast_to(pooled_slope[:, None, :], (count, PATCHES, width))
    layer_slope = layer_slope.reshape(count * PATCHES, width).astype(jnp.bfloat16)
    attended_slope = jnp.dot(layer_slope, out_whole, preferred_element_type=jnp.float32).astype(
        jnp.bfloat16
    )
    triple_slope = jax.vjp(attend, triple)[1](attended_slope)[0]
    contract_first = (((0,), (0,)), ((), ()))
    first = lax.dot_general(
        normed, triple_slope, contract_first, preferred_element_type=jnp.float32
    )
    second = lax.dot_general(
        layer_slope, attended, contract_first, preferred_element_type=jnp.float32
    )
    shard = lax.psum_scatter(
        jnp.concatenate([first, second], axis=1).astype(jnp.bfloat16),
        "dp",
        scatter_dimension=0,
        tiled=True,
    ).astype(jnp.float32)
    shard = lax.psum(shard.astype(jnp.bfloat16), "vol").astype(jnp.float32)
    split = project_in.shape[1]
    return (errors, shard[:, :split], shard[:, split:], head_gradient)


def solution(mesh):
    placed = (
        P(("dp", "vol"), None, None),
        P(("dp", "vol"), None, None),
        P("vol", None, None),
        P("dp", None, None),
        P(),
        P(),
        P(),
        P("dp", None),
        P("dp", None),
        P(),
    )
    return jax.shard_map(
        local,
        mesh=mesh,
        in_specs=placed,
        out_specs=(P(("dp", "vol"), None), P("dp", None), P("dp", None), P()),
        check_vma=False,
    )
```

profile of v0, /device:TPU:0, one launch (start us, length us, event | category | flops | bytes accessed | tf_op | source)
XLA Modules:
  0.0 261.4 jit_solution(18446166115794627641)
XLA Ops:
  8.1 0.7 fusion.38
  8.8 0.7 compare_and_fusion.1
  9.5 11.4 %gather_fusion = bf16[1024,256]{1,0:T(8,128)(2,1)S(1)} fusion(bf16[32768,256]{1,0:T(8,128)(2,1)} %bitcast.106, s32[1024]{0:T(1024)S(1)} %broadcast_clamp_fusion), kind=kCustom, calls=%fused_computation | custom fusion | bytes 1052672 | tf_op jit(solution)/shard_map/jit(_take)/gather | solution.py:67
  21.2 10.3 %slice.21 = bf16[1024,128]{1,0:T(8,128)(2,1)S(1)} slice(bf16[1024,256]{1,0:T(8,128)(2,1)S(1)} %broadcast_select_fusion), slice={[0:1024:1], [0:256:2]} | slice | bytes 524288 | tf_op jit(solution)/shard_map/slice | solution.py:67
  31.7 0.8 convert_element_type.102
  35.0 0.6 fusion.24
  35.6 0.6 convert_element_type.105
  37.5 0.6 dynamic-slice
  38.1 0.6 fusion.9
  38.7 19.9 %all-reduce.9.cloned.1.call-done = bf16[2,65536]{1,0:T(2,128)(2,1)} async-done(((bf16[2,65536]{1,0:T(2,128)(2,1)}), bf16[2,65536]{1,0:T(2,128)(2,1)}) %all-reduce.9.cloned.1.call-update) | async-done | bytes 262160
  58.6 1.8 dynamic-slice_convert_fusion
  60.4 0.6 multiply_reduce_fusion
  61.0 22.6 %all-gather.3.cloned.1.call-done = bf16[1024,1536]{1,0:T(8,128)(2,1)} async-done(((bf16[64,1536]{1,0:T(8,128)(2,1)}), bf16[1024,1536]{1,0:T(8,128)(2,1)}) %all-gather.3.cloned.1.call-update) | async-done | bytes 3145744 | tf_op jit(solution)/shard_map/all_gather | solution.py:99
  83.7 3.0 %convolution_convert_fusion.1 = bf16[256,1536]{1,0:T(8,128)(2,1)S(1)} fusion(bf16[1024,1536]{1,0:T(8,128)(2,1)} %all-gather.3.cloned.1.call-done, bf16[256,1024]{1,0:T(8,128)(2,1)S(1)} %get-tuple-element.9, f32[1024]{0:T(1024)S(1)} %copy-done.17, f32[256]{0:T(256)S(1)} %add_rsqrt_fusion, f32[256]{0:T(256)S(1)} %broadcast_multiply_fusion.2), kind=kOutput, calls=%fused_computation.5 | convolution fusion | flops 807010304 | bytes 4462592 | tf_op jit(solution)/shard_map/dot_general | solution.py:97
  88.0 1.2 convolution_convert_fusion.5
  89.3 32.9 %all-gather.5.cloned.1.call-done = bf16[1024,512]{1,0:T(8,128)(2,1)} async-done(((bf16[64,512]{1,0:T(8,128)(2,1)}), bf16[1024,512]{1,0:T(8,128)(2,1)}) %all-gather.5.cloned.1.call-update) | async-done | bytes 1048592 | tf_op jit(solution)/shard_map/all_gather | solution.py:104
  122.2 1.9 fusion.8
  124.2 0.8 fusion.64
  125.0 1.3 multiply_reduce_fusion.1
  126.3 1.2 subtract_multiply_fusion
  128.1 1.5 convolution_convert_fusion.3
  129.6 1.1 convolution_convert_fusion.4
  130.7 1.1 copy.34
  131.8 1.5 fusion.4
  133.4 0.6 convolution_bitcast_fusion
  134.0 0.6 convolution_bitcast_fusion.1
  135.6 1.2 convolution_convert_fusion
  136.8 2.6 pad_maximum_fusion
  139.5 71.4 %reduce-scatter.2.cloned.1.call-done = bf16[64,2048]{1,0:T(8,128)(2,1)} async-done(((bf16[1024,2048]{1,0:T(8,128)(2,1)}), bf16[64,2048]{1,0:T(8,128)(2,1)}) %reduce-scatter.2.cloned.1.call-update) | async-done | bytes 262160 | tf_op jit(solution)/shard_map/reduce_scatter | solution.py:128
  211.0 39.6 %psum.15 = f32[1024,4]{0,1:T(4,128)} all-reduce(f32[1024,4]{0,1:T(4,128)S(1)} %broadcast_multiply_fusion), channel_id=1, replica_groups=mesh['dp'=16,'vol'=2] {'dp','vol'}, use_global_device_ids=true, to_apply=%region_11.12 | all-reduce | flops 4096 | bytes 32768 | tf_op jit(solution)/shard_map/psum | solution.py:113
  250.6 1.7 slice.32
  252.3 1.5 slice.33
  (84 shorter events, 7.3 us)
Async XLA Ops:
  8.0 28.7 %copy-start = (bf16[64,1024]{1,0:T(8,128)(2,1)S(1)}, bf16[64,1024]{1,0:T(8,128)(2,1)}, u32[]{:S(2)}) copy-start(bf16[64,1024]{1,0:T(8,128)(2,1)} %param.14) | copy-start | bytes 393220
  8.0 50.5 %all-reduce.9.cloned.1.call-start = ((), (), s32[]{:S(2)}) async-start(), calls=%async_computation.5 | async-start | bytes 524288
  20.9 13.0 %copy-start.7 = (f32[1,128,128]{2,1,0:T(8,128)S(1)}, f32[1,128,128]{2,1,0:T(8,128)}, u32[]{:S(2)}) copy-start(f32[1,128,128]{2,1,0:T(8,128)} %param.10) | copy-start | bytes 196612
  21.0 14.6 %copy-start.8 = (bf16[1,128,128]{2,1,0:T(8,128)(2,1)S(1)}, bf16[1,128,128]{2,1,0:T(8,128)(2,1)}, u32[]{:S(2)}) copy-start(bf16[1,128,128]{2,1,0:T(8,128)(2,1)} %param.11) | copy-start | bytes 98308
  31.5 5.3 %copy-start.6 = (bf16[256,1024]{1,0:T(8,128)(2,1)S(1)}, bf16[256,1024]{1,0:T(8,128)(2,1)}, u32[]{:S(2)}) copy-start(bf16[256,1024]{1,0:T(8,128)(2,1)} %param.15) | copy-start | bytes 1572868
  32.5 51.2 %all-gather.3.cloned.1.call-start = ((), (), s32[]{:S(2)}) async-start(), calls=%async_computation.1 | async-start | bytes 3342336 | tf_op jit(solution)/shard_map/all_gather | solution.py:99
  33.1 89.2 %all-gather.5.cloned.1.call-start = ((), (), s32[]{:S(2)}) async-start(), calls=%async_computation.2 | async-start | bytes 1114112 | tf_op jit(solution)/shard_map/all_gather | solution.py:104
  33.6 177.2 %reduce-scatter.2.cloned.1.call-start = ((), (), s32[]{:S(2)}) async-start(), calls=%async_computation.3 | async-start | bytes 4456448 | tf_op jit(solution)/shard_map/reduce_scatter | solution.py:128
  34.4 3.1 %copy-start.22 = (u32[32]{0:T(128)S(1)}, u32[32]{0:T(128)}, u32[]{:S(2)}) copy-start(u32[32]{0:T(128)} %constant.104) | copy-start | bytes 388
  36.2 47.5 %copy-start.17 = (f32[1024]{0:T(1024)S(1)}, f32[1024]{0:T(1024)}, u32[]{:S(2)}) copy-start(f32[1024]{0:T(1024)} %param.16) | copy-start | bytes 12292
  37.2 49.5 %copy-start.1 = (bf16[256,1024]{1,0:T(8,128)(2,1)}, bf16[256,1024]{1,0:T(8,128)(2,1)S(1)}, u32[]{:S(2)}) copy-start(bf16[256,1024]{1,0:T(8,128)(2,1)S(1)} %get-tuple-element.9) | copy-start | bytes 1572868
  37.2 49.5 %copy-start.12 = (f32[256]{0:T(256)}, f32[256]{0:T(256)S(1)}, u32[]{:S(2)}) copy-start(f32[256]{0:T(256)S(1)} %broadcast_multiply_fusion.2) | copy-start | bytes 3076
  37.5 49.2 %copy-start.19 = (f32[256]{0:T(256)}, f32[256]{0:T(256)S(1)}, u32[]{:S(2)}) copy-start(f32[256]{0:T(256)S(1)} %add_rsqrt_fusion) | copy-start | bytes 3076
  87.0 0.9 copy-start.3
  122.2 2.0 copy-start.9
  122.2 2.8 %copy-start.14 = (f32[4]{0:T(128)S(1)}, f32[4]{0:T(128)}, u32[]{:S(2)}) copy-start(f32[4]{0:T(128)} %multiply_reduce_fusion) | copy-start | bytes 52
  122.2 7.4 %copy-start.21 = (bf16[1024,512]{1,0:T(8,128)(2,1)S(1)}, bf16[1024,512]{1,0:T(8,128)(2,1)}, u32[]{:S(2)}) copy-start(bf16[1024,512]{1,0:T(8,128)(2,1)} %all-gather.5.cloned.1.call-done) | copy-start | bytes 3145732
  124.2 3.5 %copy-start.10 = (f32[1024]{0:T(1024)}, f32[1024]{0:T(1024)S(1)}, u32[]{:S(2)}) copy-start(f32[1024]{0:T(1024)S(1)} %broadcast_multiply_fusion.1) | copy-start | bytes 12292
  127.5 0.6 copy-start.15
  131.8 1.6 copy-start.4
  134.6 1.0 copy-start.2
  134.6 1.0 copy-start.13
  134.6 1.0 copy-start.18
  134.6 1.0 copy-start.20
  135.6 1.2 copy-start.5
  139.4 71.5 %copy-start.11 = (f32[1024]{0:T(1024)S(1)}, f32[1024]{0:T(1024)}, u32[]{:S(2)}) copy-start(f32[1024]{0:T(1024)} %copy-done.10) | copy-start | bytes 12292
  139.4 71.5 %copy-start.16 = (f32[4]{0:T(128)S(1)}, f32[4]{0:T(128)}, u32[]{:S(2)}) copy-start(f32[4]{0:T(128)} %copy-done.15) | copy-start | bytes 52
  139.4 111.2 %all-reduce.7.cloned.1.call-start = ((), (), s32[]{:S(2)}) async-start(), calls=%async_computation.4 | async-start | bytes 524288 | tf_op jit(solution)/shard_map/psum | solution.py:134
Sparse Core Ops, SparseCore 0:
  32.6 25.9 all-reduce.8
  211.0 22.3 all-reduce.6
Sparse Core Ops, SparseCore 1:
  35.5 48.1 all-gather.2
  85.9 36.2 all-gather.4
  139.5 71.3 reduce-scatter.1
where the time goes:
time: 262 us; the launch traced here: 261 us
  waiting for transfers between devices  148 us (56%)
  blocking collectives  39.6 us (15%)
  local copies, waits for them, and re-layouts  30.1 us (11%)
  matrix products  17.1 us (7%)
  between operations  16.1 us (6%)
  other arithmetic  10.1 us (4%)
    reduce_scatter x1, waiting for transfers between devices, local(): lax.psum_scatter(jnp.concatenate([first, second], axis=1).astype(jnp.bflo...  71.4 us
    psum x1, blocking collectives, local(): lax.psum(jnp.dot(pooled.T, logit_slope, precision=highest), ('dp', 'vol'))  39.6 us
    all_gather x1, waiting for transfers between devices, local(): out_whole = lax.all_gather(project_out, 'dp', axis=0, tiled=True)  32.9 us
    all_gather x1, waiting for transfers between devices, local(): lax.all_gather(project_in, 'dp', axis=0, tiled=True)  22.6 us
    unnamed x6, waiting for transfers between devices  21 us
    gather x1, local copies, waits for them, and re-layouts, render(): picked = jnp.take(table, rows.reshape(-1), axis=0)[:, ::2]  11.4 us
    slice x1, local copies, waits for them, and re-layouts, render(): picked = jnp.take(table, rows.reshape(-1), axis=0)[:, ::2]  10.3 us
  transfers between devices with their start and end apart: 5, of which 4 were waited for; matrix products, arithmetic and copies ran while one was open for 5% of the time, Pallas kernels for 0%

commit v1 on v0

--- a/solution.py
+++ b/solution.py
@@ -11,6 +11,18 @@
 PATCHES = 256
 K = 4
 EPSILON = 1e-05
+
+
+def collect(x, axis, dim):
+    ways, here, step = (lax.axis_size(axis), lax.axis_index(axis), x.shape[dim])
+    line, have = (x, 1)
+    while have < ways:
+        line = jnp.concatenate(
+            [line, lax.ppermute(line, axis, [(d, (d - have) % ways) for d in range(ways)])],
+            axis=dim,
+        )
+        have = 2 * have
+    return jnp.roll(line, here * step, axis=dim)
 
 
 def embed_images(images, patch_weight, position):
@@ -101,7 +113,7 @@
     ).astype(jnp.bfloat16)
     attended = attend(triple)
     contract_last = (((1,), (1,)), ((), ()))
-    out_whole = lax.all_gather(project_out, "dp", axis=0, tiled=True)
+    out_whole = collect(project_out, "dp", 0)
     branch = lax.dot_general(attended, out_whole, contract_last, preferred_element_type=jnp.float32)
     layer_out = embedded.astype(jnp.float32) + branch
     pooled = jnp.mean(layer_out.reshape(count, PATCHES, width), axis=1)

time: 262 us -> 250 us (0.954)
  waiting for transfers between devices: 148 us -> 121 us
  starting transfers between devices: 0.39 us -> 9.74 us
  local copies, waits for them, and re-layouts: 30.1 us -> 37.3 us
    ppermute x0 -> x4, waiting for transfers between devices: none -> 46.7 us  [collect(): lax.ppermute(line, axis, [(d, (d - have) % ways) for d in range(ways)])]
    all_gather x1 -> x0, waiting for transfers between devices: 32.9 us -> none  [local(): out_whole = lax.all_gather(project_out, 'dp', axis=0, tiled=True)]
    all_gather x1, waiting for transfers between devices: 22.6 us -> 0.01 us  [local(): lax.all_gather(project_in, 'dp', axis=0, tiled=True)]
    unnamed x6 -> x5, waiting for transfers between devices: 21 us -> 0.07 us
    ppermute x0 -> x4, starting transfers between devices: none -> 9.57 us  [collect(): lax.ppermute(line, axis, [(d, (d - have) % ways) for d in range(ways)])]
    unnamed x47 -> x58, local copies, waits for them, and re-layouts: 1.93 us -> 8.33 us
    reduce_scatter x1, waiting for transfers between devices: 71.4 us -> 74.7 us  [local(): lax.psum_scatter(jnp.concatenate([first, second], axis=1).astype(jnp.bflo...]
  transfers between devices with their start and end apart: 5 -> 8, of which waited for: 4 -> 4; matrix products, arithmetic and copies ran while one was open for 5% -> 5% of each run, Pallas kernels for 0% -> 0%
where the time goes in v1:
time: 250 us; the launch traced here: 249 us
  waiting for transfers between devices  121 us (48%)
  blocking collectives  39.6 us (16%)
  local copies, waits for them, and re-layouts  37.3 us (15%)
  between operations  16 us (6%)
  matrix products  15.8 us (6%)
  starting transfers between devices  9.74 us (4%)
  other arithmetic  9.55 us (4%)
    reduce_scatter x1, waiting for transfers between devices, local(): lax.psum_scatter(jnp.concatenate([first, second], axis=1).astype(jnp.bflo...  74.7 us
    ppermute x4, waiting for transfers between devices, collect(): lax.ppermute(line, axis, [(d, (d - have) % ways) for d in range(ways)])  46.7 us
    psum x1, blocking collectives, local(): lax.psum(jnp.dot(pooled.T, logit_slope, precision=highest), ('dp', 'vol'))  39.6 us
    gather x1, local copies, waits for them, and re-layouts, render(): picked = jnp.take(table, rows.reshape(-1), axis=0)[:, ::2]  11.4 us
    slice x1, local copies, waits for them, and re-layouts, render(): picked = jnp.take(table, rows.reshape(-1), axis=0)[:, ::2]  10.3 us
    ppermute x4, starting transfers between devices, collect(): lax.ppermute(line, axis, [(d, (d - have) % ways) for d in range(ways)])  9.57 us
    unnamed x58, local copies, waits for them, and re-layouts  8.33 us
  transfers between devices with their start and end apart: 8, of which 4 were waited for; matrix products, arithmetic and copies ran while one was open for 5% of the time, Pallas kernels for 0%

profile of v1, /device:TPU:0, one launch (start us, length us, event | category | flops | bytes accessed | tf_op | source)
XLA Modules:
  0.0 249.4 jit_solution(2746393875910443105)
XLA Ops:
  8.8 0.7 fusion.40
  9.5 11.4 %gather_fusion = bf16[1024,256]{1,0:T(8,128)(2,1)S(1)} fusion(bf16[32768,256]{1,0:T(8,128)(2,1)} %bitcast.104, s32[1024]{0:T(1024)S(1)} %broadcast_clamp_fusion), kind=kCustom, calls=%fused_computation | custom fusion | bytes 1052672 | tf_op jit(solution)/shard_map/jit(_take)/gather | solution.py:79
  21.2 10.3 %slice.21 = bf16[1024,128]{1,0:T(8,128)(2,1)S(1)} slice(bf16[1024,256]{1,0:T(8,128)(2,1)S(1)} %broadcast_select_fusion), slice={[0:1024:1], [0:256:2]} | slice | bytes 524288 | tf_op jit(solution)/shard_map/slice | solution.py:79
  31.7 0.8 convert_element_type.102
  32.5 5.5 %collective-permute-start = (bf16[64,512]{1,0:T(8,128)(2,1)S(1)}, bf16[64,512]{1,0:T(8,128)(2,1)S(1)}, u32[]{:S(2)}, u32[]{:S(2)}) collective-permute-start(bf16[64,512]{1,0:T(8,128)(2,1)S(1)} %copy-done.7), channel_id=1, source_target_pairs={{0,30},{2,0},{4,2},{6,4},{8,6},{10,8},{12,10},{14,12},{16,14},{18,... | collective-permute-start | bytes 196616 | tf_op jit(solution)/shard_map/ppermute | solution.py:21
  42.2 1.1 collective-permute-start.1
  43.3 4.0 %collective-permute-done.1 = bf16[128,512]{1,0:T(8,128)(2,1)S(1)} collective-permute-done((bf16[128,512]{1,0:T(8,128)(2,1)S(1)}, bf16[128,512]{1,0:T(8,128)(2,1)S(1)}, u32[]{:S(2)}, u32[]{:S(2)}) %collective-permute-start.1) | collective-permute-done | bytes 131104 | tf_op jit(solution)/shard_map/ppermute | solution.py:21
  47.3 2.0 collective-permute-start.2
  51.8 9.3 %collective-permute-done.2 = bf16[256,512]{1,0:T(8,128)(2,1)S(1)} collective-permute-done((bf16[256,512]{1,0:T(8,128)(2,1)S(1)}, bf16[256,512]{1,0:T(8,128)(2,1)S(1)}, u32[]{:S(2)}, u32[]{:S(2)}) %collective-permute-start.2) | collective-permute-done | bytes 262176 | tf_op jit(solution)/shard_map/ppermute | solution.py:21
  61.1 1.0 collective-permute-start.3
  62.1 1.8 dynamic-slice_convert_fusion
  64.1 0.7 constant_dynamic-update-slice_fusion.6
  64.8 33.5 %collective-permute-done.3 = bf16[512,512]{1,0:T(8,128)(2,1)S(1)} collective-permute-done((bf16[512,512]{1,0:T(8,128)(2,1)S(1)}, bf16[512,512]{1,0:T(8,128)(2,1)S(1)}, u32[]{:S(2)}, u32[]{:S(2)}) %collective-permute-start.3) | collective-permute-done | bytes 524320 | tf_op jit(solution)/shard_map/ppermute | solution.py:21
  98.3 0.8 constant_dynamic-update-slice_fusion.5
  101.1 0.7 constant_dynamic-update-slice_fusion.1
  101.8 0.8 constant_dynamic-update-slice_fusion
  102.6 3.0 %convolution_convert_fusion.1 = bf16[256,1536]{1,0:T(8,128)(2,1)S(1)} fusion(bf16[1024,1536]{1,0:T(8,128)(2,1)} %all-gather.2.cloned.1.call-done, bf16[256,1024]{1,0:T(8,128)(2,1)S(1)} %get-tuple-element.9, f32[1024]{0:T(1024)S(1)} %copy-done.18, f32[256]{0:T(256)S(1)} %add_rsqrt_fusion, f32[256]{0:T(256)S(1)} %broadcast_multiply_fusion.2), kind=kOutput, calls=%fused_computation.5 | convolution fusion | flops 807010304 | bytes 4462592 | tf_op jit(solution)/shard_map/dot_general | solution.py:109
  107.0 1.4 convolution_convert_fusion.5
  109.2 0.8 fusion.68
  110.0 1.2 multiply_reduce_fusion.1
  111.2 1.2 subtract_multiply_fusion
  112.6 1.1 convolution_convert_fusion.4
  113.7 1.5 convolution_convert_fusion.3
  115.2 1.1 copy.34
  116.7 1.5 fusion.4
  119.6 0.9 copy-done.3
  120.5 1.2 convolution_convert_fusion
  121.7 2.6 %pad_maximum_fusion = bf16[1024,2048]{1,0:T(8,128)(2,1)} fusion(bf16[1024,512]{1,0:T(8,128)(2,1)S(1)} %copy-done.6, bf16[1024,1536]{1,0:T(8,128)(2,1)S(1)} %convolution_convert_fusion), kind=kLoop, calls=%fused_computation.1 | loop fusion | flops 8388608 | bytes 8388608 | tf_op jit(solution)/shard_map/concatenate | solution.py:141
  124.4 74.7 %reduce-scatter.2.cloned.1.call-done = bf16[64,2048]{1,0:T(8,128)(2,1)} async-done(((bf16[1024,2048]{1,0:T(8,128)(2,1)}), bf16[64,2048]{1,0:T(8,128)(2,1)}) %reduce-scatter.2.cloned.1.call-update) | async-done | bytes 262160 | tf_op jit(solution)/shard_map/reduce_scatter | solution.py:140
  199.2 39.6 %psum.15 = f32[1024,4]{0,1:T(4,128)} all-reduce(f32[1024,4]{0,1:T(4,128)S(1)} %broadcast_multiply_fusion), channel_id=1, replica_groups=mesh['dp'=16,'vol'=2] {'dp','vol'}, use_global_device_ids=true, to_apply=%region_11.12 | all-reduce | flops 4096 | bytes 32768 | tf_op jit(solution)/shard_map/psum | solution.py:125
  238.8 1.5 slice.33
  240.3 1.7 slice.32
  (104 shorter events, 14.2 us)
Async XLA Ops:
  8.0 32.9 %copy-start = (bf16[64,1024]{1,0:T(8,128)(2,1)S(1)}, bf16[64,1024]{1,0:T(8,128)(2,1)}, u32[]{:S(2)}) copy-start(bf16[64,1024]{1,0:T(8,128)(2,1)} %param.14) | copy-start | bytes 393220
  8.0 54.1 %all-reduce.9.cloned.1.call-start = ((), (), s32[]{:S(2)}) async-start(), calls=%async_computation.4 | async-start | bytes 524288
  20.9 11.6 %copy-start.7 = (bf16[64,512]{1,0:T(8,128)(2,1)S(1)}, bf16[64,512]{1,0:T(8,128)(2,1)}, u32[]{:S(2)}) copy-start(bf16[64,512]{1,0:T(8,128)(2,1)} %param.18) | copy-start | bytes 196612
  20.9 17.2 %copy-start.9 = (f32[1,128,128]{2,1,0:T(8,128)S(1)}, f32[1,128,128]{2,1,0:T(8,128)}, u32[]{:S(2)}) copy-start(f32[1,128,128]{2,1,0:T(8,128)} %param.10) | copy-start | bytes 196612
  20.9 18.8 %copy-start.10 = (bf16[1,128,128]{2,1,0:T(8,128)(2,1)S(1)}, bf16[1,128,128]{2,1,0:T(8,128)(2,1)}, u32[]{:S(2)}) copy-start(bf16[1,128,128]{2,1,0:T(8,128)(2,1)} %param.11) | copy-start | bytes 98308
  31.4 9.5 %copy-start.8 = (bf16[256,1024]{1,0:T(8,128)(2,1)S(1)}, bf16[256,1024]{1,0:T(8,128)(2,1)}, u32[]{:S(2)}) copy-start(bf16[256,1024]{1,0:T(8,128)(2,1)} %param.15) | copy-start | bytes 1572868
  32.5 70.2 %all-gather.2.cloned.1.call-start = ((), (), s32[]{:S(2)}) async-start(), calls=%async_computation.1 | async-start | bytes 3342336 | tf_op jit(solution)/shard_map/all_gather | solution.py:111
  32.5 9.7 %collective-permute-start = (bf16[64,512]{1,0:T(8,128)(2,1)S(1)}, bf16[64,512]{1,0:T(8,128)(2,1)S(1)}, u32[]{:S(2)}, u32[]{:S(2)}) collective-permute-start(bf16[64,512]{1,0:T(8,128)(2,1)S(1)} %copy-done.7), channel_id=1, source_target_pairs={{0,30},{2,0},{4,2},{6,4},{8,6},{10,8},{12,10},{14,12},{16,14},{18,... | collective-permute-start | bytes 196616 | tf_op jit(solution)/shard_map/ppermute | solution.py:21
  38.0 161.1 %reduce-scatter.2.cloned.1.call-start = ((), (), s32[]{:S(2)}) async-start(), calls=%async_computation.2 | async-start | bytes 4456448 | tf_op jit(solution)/shard_map/reduce_scatter | solution.py:140
  40.3 9.6 %copy-start.23 = (u32[32]{0:T(128)S(1)}, u32[32]{0:T(128)}, u32[]{:S(2)}) copy-start(u32[32]{0:T(128)} %constant.131) | copy-start | bytes 388
  41.3 61.3 %copy-start.1 = (bf16[256,1024]{1,0:T(8,128)(2,1)}, bf16[256,1024]{1,0:T(8,128)(2,1)S(1)}, u32[]{:S(2)}) copy-start(bf16[256,1024]{1,0:T(8,128)(2,1)S(1)} %get-tuple-element.9) | copy-start | bytes 1572868
  41.3 61.3 %copy-start.14 = (f32[256]{0:T(256)}, f32[256]{0:T(256)S(1)}, u32[]{:S(2)}) copy-start(f32[256]{0:T(256)S(1)} %broadcast_multiply_fusion.2) | copy-start | bytes 3076
  42.2 5.0 %collective-permute-start.1 = (bf16[128,512]{1,0:T(8,128)(2,1)S(1)}, bf16[128,512]{1,0:T(8,128)(2,1)S(1)}, u32[]{:S(2)}, u32[]{:S(2)}) collective-permute-start(bf16[128,512]{1,0:T(8,128)(2,1)S(1)} %pad_maximum_fusion.3), channel_id=1, source_target_pairs={{0,28},{2,30},{4,0},{6,2},{8,4},{10,6},{12,8},{14,10},{16,12},{18,... | collective-permute-start | bytes 393224 | tf_op jit(solution)/shard_map/ppermute | solution.py:21
  43.3 59.3 %copy-start.20 = (f32[256]{0:T(256)}, f32[256]{0:T(256)S(1)}, u32[]{:S(2)}) copy-start(f32[256]{0:T(256)S(1)} %add_rsqrt_fusion) | copy-start | bytes 3076
  47.3 13.8 %collective-permute-start.2 = (bf16[256,512]{1,0:T(8,128)(2,1)S(1)}, bf16[256,512]{1,0:T(8,128)(2,1)S(1)}, u32[]{:S(2)}, u32[]{:S(2)}) collective-permute-start(bf16[256,512]{1,0:T(8,128)(2,1)S(1)} %pad_maximum_fusion.2), channel_id=1, source_target_pairs={{0,24},{2,26},{4,28},{6,30},{8,0},{10,2},{12,4},{14,6},{16,8},{18,... | collective-permute-start | bytes 786440 | tf_op jit(solution)/shard_map/ppermute | solution.py:21
  61.1 37.2 %collective-permute-start.3 = (bf16[512,512]{1,0:T(8,128)(2,1)S(1)}, bf16[512,512]{1,0:T(8,128)(2,1)S(1)}, u32[]{:S(2)}, u32[]{:S(2)}) collective-permute-start(bf16[512,512]{1,0:T(8,128)(2,1)S(1)} %pad_maximum_fusion.1), channel_id=1, source_target_pairs={{0,16},{2,18},{4,20},{6,22},{8,24},{10,26},{12,28},{14,30},{16,0},... | collective-permute-start | bytes 1572872 | tf_op jit(solution)/shard_map/ppermute | solution.py:21
  64.0 38.7 %copy-start.18 = (f32[1024]{0:T(1024)S(1)}, f32[1024]{0:T(1024)}, u32[]{:S(2)}) copy-start(f32[1024]{0:T(1024)} %param.16) | copy-start | bytes 12292
  105.9 0.9 copy-start.4
  106.8 1.6 copy-start.2
  106.8 1.8 copy-start.22
  107.0 2.2 copy-start.11
  109.2 4.5 %copy-start.12 = (f32[1024]{0:T(1024)}, f32[1024]{0:T(1024)S(1)}, u32[]{:S(2)}) copy-start(f32[1024]{0:T(1024)S(1)} %broadcast_multiply_fusion.1) | copy-start | bytes 12292
  112.4 1.3 copy-start.16
  116.7 1.6 copy-start.5
  119.5 1.0 copy-start.3
  119.5 1.0 copy-start.15
  119.5 1.0 copy-start.19
  119.5 1.0 copy-start.21
  120.5 1.2 copy-start.6
  124.3 74.8 %copy-start.13 = (f32[1024]{0:T(1024)S(1)}, f32[1024]{0:T(1024)}, u32[]{:S(2)}) copy-start(f32[1024]{0:T(1024)} %copy-done.12) | copy-start | bytes 12292
  124.3 74.8 %copy-start.17 = (f32[4]{0:T(128)S(1)}, f32[4]{0:T(128)}, u32[]{:S(2)}) copy-start(f32[4]{0:T(128)} %copy-done.16) | copy-start | bytes 52
  124.4 114.4 %all-reduce.7.cloned.1.call-start = ((), (), s32[]{:S(2)}) async-start(), calls=%async_computation.3 | async-start | bytes 524288 | tf_op jit(solution)/shard_map/psum | solution.py:146
Sparse Core Ops, SparseCore 0:
  32.6 25.9 all-reduce.8
  199.2 22.3 all-reduce.6
Sparse Core Ops, SparseCore 1:
  38.1 57.0 all-gather.1
  124.5 74.6 reduce-scatter.1
